TPU v7x, 32 devices: a whole 2x2x4 slice. The times are simulated.
32 devices in a mesh: dp: 8 (over z, x), mp: 4 (over y, core).
Axes of the slice: x: 2, y: 2, z: 4, core: 2. Of those that a mesh axis runs over, the one named last changes fastest.
Arguments:
- tokens: bfloat16 [16, 1024, 1024], P('dp', 'mp'), may hold values from -6 to 6
- lengths: int32 [16], P('dp'), may hold values from 256 to 1024, as said below
- attn_norm: bfloat16 [1024], P('dp'), may hold values from 0.099609375 to 1.8984375
- qkv_weight: bfloat16 [3, 1024, 1024], P(None, 'dp', 'mp'), may hold values from -0.25 to 0.25
- attn_out_weight: bfloat16 [1024, 1024], P('mp', 'dp'), may hold values from -1.5 to 1.5
- ffn_norm: bfloat16 [1024], P('dp'), may hold values from 0.099609375 to 1.8984375
- ffn_in_weight: bfloat16 [2, 1024, 2624], P(None, 'dp', 'mp'), may hold values from -0.1875 to 0.1875
- ffn_out_weight: bfloat16 [2624, 1024], P('mp', 'dp'), may hold values from -0.125 to 0.125
- out_grad: bfloat16 [16, 1024, 1024], P('dp', 'mp'), may hold values from -6 to 6
Outputs:
- output: bfloat16 [16, 1024, 1024], P('dp', 'mp')
- grad_input: bfloat16 [16, 1024, 1024], P('dp', 'mp')
- grad_attn_norm: float32 [1024], P('dp')
- grad_qkv: float32 [3, 1024, 1024], P(None, 'dp', 'mp')
- grad_attn_out: float32 [1024, 1024], P('mp', 'dp')
- grad_ffn_norm: float32 [1024], P('dp')
- grad_ffn_in: float32 [2, 1024, 2624], P(None, 'dp', 'mp')
- grad_ffn_out: float32 [2624, 1024], P('mp', 'dp')
Inputs may be any that keep to these rules, and one draw needn't show every extreme that they name: Sequence s holds valid tokens at positions 0 to lengths[s] - 1 and padding after; some sequence has exactly 1024 and some exactly 256.
All inputs are finite; a program needn't handle non-finite values.
Results may differ from a plain program's by a relative error of at most 0.02.
Values may be sent and summed in bfloat16 or wider, within the bound.
No kernel may reach another device: no remote copies, remote signals or barrier semaphores. Data moves between devices by JAX's collectives and lax.ppermute only.
A program may use at most 192 MiB of HBM per device.

v0:
```python
import jax
import jax.numpy as jnp
from jax import lax
from jax.sharding import PartitionSpec as P

HD = 64
norm_eps = 1e-05
rope_base = 160000.0


def layer_norm(values, norm_gain):
    average = jnp.mean(values, axis=-1, keepdims=True)
    centred = values - average
    spread = jnp.mean(centred * centred, axis=-1, keepdims=True)
    return centred * lax.rsqrt(spread + norm_eps) * norm_gain


def rope_tables(length, head_size):
    places = jnp.arange(length, dtype=jnp.float32)
    frequency = rope_base ** (-jnp.arange(0, head_size, 2, dtype=jnp.float32) / head_size)
    angles = places[:, None] * frequency[None, :]
    angles = jnp.concatenate([angles, angles], axis=-1)
    return (jnp.cos(angles), jnp.sin(angles))


def rotate(values, cosine_table, sine_table):
    half_size = values.shape[-1] // 2
    turned = jnp.concatenate([-values[..., half_size:], values[..., :half_size]], axis=-1)
    return values * cosine_table + turned * sine_table


def unrotate(grad_rows, cosine_table, sine_table):
    half_size = grad_rows.shape[-1] // 2
    scaled = grad_rows * sine_table
    return grad_rows * cosine_table + jnp.concatenate(
        [scaled[..., half_size:], -scaled[..., :half_size]], axis=-1
    )


def gelu_product(up_rows, gate_rows):
    return jax.nn.gelu(up_rows, approximate=False) * gate_rows


def masked_scores(query_rows, key_rows, key_valid, score_scale):
    scores = (
        jnp.einsum("qhd,khd->hqk", query_rows, key_rows, preferred_element_type=jnp.float32)
        * score_scale
    )
    return jnp.where(key_valid[None, None, :], scores, -jnp.inf)


def fetch_attention(qkv_weight, attn_out_weight, attn_norm):
    return (
        lax.all_gather(qkv_weight, "dp", axis=1, tiled=True),
        lax.all_gather(attn_out_weight, "dp", axis=1, tiled=True),
        lax.all_gather(attn_norm, "dp", axis=0, tiled=True),
    )


def fetch_feedforward(ffn_in_weight, ffn_out_weight, ffn_norm):
    return (
        lax.all_gather(ffn_in_weight, "dp", axis=1, tiled=True),
        lax.all_gather(ffn_out_weight, "dp", axis=1, tiled=True),
        lax.all_gather(ffn_norm, "dp", axis=0, tiled=True),
    )


def fetch_attention_again(qkv_weight, attn_out_weight, attn_norm):
    return (
        lax.all_gather(qkv_weight, "dp", axis=1, tiled=True),
        lax.all_gather(attn_out_weight, "dp", axis=1, tiled=True),
        lax.all_gather(attn_norm, "dp", axis=0, tiled=True),
    )


def fetch_feedforward_again(ffn_in_weight, ffn_out_weight, ffn_norm):
    return (
        lax.all_gather(ffn_in_weight, "dp", axis=1, tiled=True),
        lax.all_gather(ffn_out_weight, "dp", axis=1, tiled=True),
        lax.all_gather(ffn_norm, "dp", axis=0, tiled=True),
    )


def per_device(
    tokens,
    lengths,
    attn_norm,
    qkv_weight,
    attn_out_weight,
    ffn_norm,
    ffn_in_weight,
    ffn_out_weight,
    out_grad,
):
    micro_count = tokens.shape[0]
    local_len = tokens.shape[1]
    width = tokens.shape[2]
    full_len = local_len * lax.axis_size("mp")
    head_cols = qkv_weight.shape[2]
    heads_dev = head_cols // HD
    units_dev = ffn_in_weight.shape[2]
    score_scale = HD ** (-0.5)
    offset = lax.axis_index("mp") * local_len
    positions = jnp.arange(full_len, dtype=jnp.int32)
    local_positions = offset + jnp.arange(local_len, dtype=jnp.int32)
    cosine_table, sine_table = rope_tables(full_len, HD)
    cosine_table = cosine_table[:, None, :]
    sine_table = sine_table[:, None, :]
    grad_qkv = jnp.zeros((3, width, head_cols), jnp.float32)
    grad_attn_out = jnp.zeros((head_cols, width), jnp.float32)
    grad_ffn_in = jnp.zeros((2, width, units_dev), jnp.float32)
    grad_ffn_out = jnp.zeros((units_dev, width), jnp.float32)
    grad_attn_gain = jnp.zeros((width,), jnp.float32)
    grad_ffn_gain = jnp.zeros((width,), jnp.float32)
    outputs = []
    input_grads = []
    for micro_step in range(micro_count):
        qkv_full, attn_out_full, attn_gain_low = fetch_attention(
            qkv_weight, attn_out_weight, attn_norm
        )
        ffn_in_full, ffn_out_full, ffn_gain_low = fetch_feedforward(
            ffn_in_weight, ffn_out_weight, ffn_norm
        )
        attn_gain = attn_gain_low.astype(jnp.float32)
        ffn_gain = ffn_gain_low.astype(jnp.float32)
        token_rows = tokens[micro_step].astype(jnp.float32)
        seq_length = lengths[micro_step]
        row_valid = (local_positions < seq_length).astype(jnp.float32)[:, None]
        key_valid = positions < seq_length
        normed_value, first_pull = jax.vjp(layer_norm, token_rows, attn_gain)
        normed_one = normed_value.astype(jnp.bfloat16)
        full_one = lax.all_gather(normed_one, "mp", axis=0, tiled=True)
        projected = jnp.einsum(
            "ld,cde->cle", full_one, qkv_full, preferred_element_type=jnp.float32
        )
        query_rows = rotate(
            projected[0].reshape(full_len, heads_dev, HD), cosine_table, sine_table
        ).astype(jnp.bfloat16)
        key_rows = rotate(
            projected[1].reshape(full_len, heads_dev, HD), cosine_table, sine_table
        ).astype(jnp.bfloat16)
        value_rows = projected[2].reshape(full_len, heads_dev, HD).astype(jnp.bfloat16)
        scores = masked_scores(query_rows, key_rows, key_valid, score_scale)
        top_score = jnp.max(scores, axis=-1, keepdims=True)
        log_total = top_score + jnp.log(
            jnp.sum(jnp.exp(scores - top_score), axis=-1, keepdims=True)
        )
        probabilities = jnp.exp(scores - log_total).astype(jnp.bfloat16)
        context = jnp.einsum(
            "hqk,khd->qhd", probabilities, value_rows, preferred_element_type=jnp.float32
        )
        context = context.astype(jnp.bfloat16).reshape(full_len, head_cols)
        attention = lax.psum_scatter(
            jnp.dot(context, attn_out_full, preferred_element_type=jnp.float32),
            "mp",
            scatter_dimension=0,
            tiled=True,
        )
        hidden = token_rows + attention
        normed_hidden, second_pull = jax.vjp(layer_norm, hidden, ffn_gain)
        normed_two = normed_hidden.astype(jnp.bfloat16)
        full_two = lax.all_gather(normed_two, "mp", axis=0, tiled=True)
        up_gate = jnp.einsum(
            "ld,cdf->clf", full_two, ffn_in_full, preferred_element_type=jnp.float32
        )
        mixed_value, gelu_pull = jax.vjp(gelu_product, up_gate[0], up_gate[1])
        mixed_rows = mixed_value.astype(jnp.bfloat16)
        feedforward = lax.psum_scatter(
            jnp.dot(mixed_rows, ffn_out_full, preferred_element_type=jnp.float32).astype(
                jnp.bfloat16
            ),
            "mp",
            scatter_dimension=0,
            tiled=True,
        ).astype(jnp.float32)
        outputs.append((row_valid * (hidden + feedforward)).astype(jnp.bfloat16))
        qkv_full, attn_out_full, attn_gain_low = fetch_attention_again(
            qkv_weight, attn_out_weight, attn_norm
        )
        ffn_in_full, ffn_out_full, ffn_gain_low = fetch_feedforward_again(
            ffn_in_weight, ffn_out_weight, ffn_norm
        )
        out_back = row_valid * out_grad[micro_step].astype(jnp.float32)
        full_out_back = lax.all_gather(out_back.astype(jnp.bfloat16), "mp", axis=0, tiled=True)
        grad_ffn_out = grad_ffn_out + jnp.einsum(
            "lf,ld->fd", mixed_rows, full_out_back, preferred_element_type=jnp.float32
        )
        mixed_back = jnp.einsum(
            "ld,fd->lf", full_out_back, ffn_out_full, preferred_element_type=jnp.float32
        )
        up_back, gate_back = gelu_pull(mixed_back)
        up_gate_back = jnp.stack([up_back, gate_back]).astype(jnp.bfloat16)
        grad_ffn_in = grad_ffn_in + jnp.einsum(
            "ld,clf->cdf", full_two, up_gate_back, preferred_element_type=jnp.float32
        )
        normed_two_back = lax.psum_scatter(
            jnp.einsum(
                "clf,cdf->ld", up_gate_back, ffn_in_full, preferred_element_type=jnp.float32
            ).astype(jnp.bfloat16),
            "mp",
            scatter_dimension=0,
            tiled=True,
        ).astype(jnp.float32)
        hidden_norm_back, ffn_gain_part = second_pull(normed_two_back)
        grad_ffn_gain = grad_ffn_gain + ffn_gain_part
        hidden_back = out_back + hidden_norm_back
        full_hidden_back = lax.all_gather(
            hidden_back.astype(jnp.bfloat16), "mp", axis=0, tiled=True
        )
        grad_attn_out = grad_attn_out + jnp.einsum(
            "le,ld->ed", context, full_hidden_back, preferred_element_type=jnp.float32
        )
        context_back = jnp.einsum(
            "ld,ed->le", full_hidden_back, attn_out_full, preferred_element_type=jnp.float32
        )
        context_back = context_back.astype(jnp.bfloat16).reshape(full_len, heads_dev, HD)
        scores_again = masked_scores(query_rows, key_rows, key_valid, score_scale)
        probs_again = jnp.exp(scores_again - log_total)
        value_back = jnp.einsum(
            "hqk,qhd->khd",
            probs_again.astype(jnp.bfloat16),
            context_back,
            preferred_element_type=jnp.float32,
        )
        probs_back = jnp.einsum(
            "qhd,khd->hqk", context_back, value_rows, preferred_element_type=jnp.float32
        )
        row_inner = jnp.sum(probs_again * probs_back, axis=-1, keepdims=True)
        scores_back = (probs_again * (probs_back - row_inner)).astype(jnp.bfloat16)
        query_grad = (
            jnp.einsum("hqk,khd->qhd", scores_back, key_rows, preferred_element_type=jnp.float32)
            * score_scale
        )
        key_grad = (
            jnp.einsum("hqk,qhd->khd", scores_back, query_rows, preferred_element_type=jnp.float32)
            * score_scale
        )
        query_back = unrotate(query_grad, cosine_table, sine_table).astype(jnp.bfloat16)
        key_back = unrotate(key_grad, cosine_table, sine_table).astype(jnp.bfloat16)
        projected_back = jnp.stack(
            [
                query_back.reshape(full_len, head_cols),
                key_back.reshape(full_len, head_cols),
                value_back.astype(jnp.bfloat16).reshape(full_len, head_cols),
            ]
        )
        grad_qkv = grad_qkv + jnp.einsum(
            "ld,cle->cde", full_one, projected_back, preferred_element_type=jnp.float32
        )
        normed_one_back = lax.psum_scatter(
            jnp.einsum(
                "cle,cde->ld", projected_back, qkv_full, preferred_element_type=jnp.float32
            ).astype(jnp.bfloat16),
            "mp",
            scatter_dimension=0,
            tiled=True,
        ).astype(jnp.float32)
        token_back, attn_gain_part = first_pull(normed_one_back)
        grad_attn_gain = grad_attn_gain + attn_gain_part
        input_grads.append((hidden_back + token_back).astype(jnp.bfloat16))
    shards = (
        lax.psum_scatter(
            grad_qkv.astype(jnp.bfloat16), "dp", scatter_dimension=1, tiled=True
        ).astype(jnp.float32),
        lax.psum_scatter(
            grad_attn_out.astype(jnp.bfloat16), "dp", scatter_dimension=1, tiled=True
        ).astype(jnp.float32),
        lax.psum_scatter(
            grad_ffn_in.astype(jnp.bfloat16), "dp", scatter_dimension=1, tiled=True
        ).astype(jnp.float32),
        lax.psum_scatter(
            grad_ffn_out.astype(jnp.bfloat16), "dp", scatter_dimension=1, tiled=True
        ).astype(jnp.float32),
        lax.psum_scatter(
            grad_attn_gain.astype(jnp.bfloat16), "dp", scatter_dimension=0, tiled=True
        ).astype(jnp.float32),
        lax.psum_scatter(
            grad_ffn_gain.astype(jnp.bfloat16), "dp", scatter_dimension=0, tiled=True
        ).astype(jnp.float32),
    )
    attn_gain_total, ffn_gain_total = lax.psum((shards[4], shards[5]), "mp")
    return (
        jnp.stack(outputs),
        jnp.stack(input_grads),
        attn_gain_total,
        shards[0],
        shards[1],
        ffn_gain_total,
        shards[2],
        shards[3],
    )


def solution(mesh):
    in_specs = (
        P("dp", "mp", None),
        P("dp"),
        P("dp"),
        P(None, "dp", "mp"),
        P("mp", "dp"),
        P("dp"),
        P(None, "dp", "mp"),
        P("mp", "dp"),
        P("dp", "mp", None),
    )
    out_specs = (
        P("dp", "mp", None),
        P("dp", "mp", None),
        P("dp"),
        P(None, "dp", "mp"),
        P("mp", "dp"),
        P("dp"),
        P(None, "dp", "mp"),
        P("mp", "dp"),
    )
    return jax.shard_map(
        per_device, mesh=mesh, in_specs=in_specs, out_specs=out_specs, check_vma=False
    )
```

profile of v0, /device:TPU:0, one launch (start us, length us, event | category | flops | bytes accessed | tf_op | source)
XLA Modules:
  0.0 1003.6 jit_solution(15254512548151848023)
XLA Ops:
  9.1 22.3 %all-gather = bf16[8,1,128]{2,1,0:T(2,128)(2,1)S(1)} all-gather(bf16[1,1,128]{2,1,0:T(2,128)(2,1)} %bitcast.478), channel_id=1, replica_groups=mesh['dp'=8,'mp'=4] {'dp'}, dimensions={0}, use_global_device_ids=true | all-gather | bytes 2304 | tf_op jit(solution)/shard_map/all_gather | solution.py:56
  40.3 30.8 %all_gather.59 = bf16[256,1024]{1,0:T(8,128)(2,1)} all-gather(bf16[256,128]{1,0:T(8,128)(2,1)S(1)} %copy-done.60), channel_id=1, replica_groups=mesh['dp'=8,'mp'=4] {'dp'}, dimensions={1}, use_global_device_ids=true | all-gather | bytes 589824 | tf_op jit(solution)/shard_map/all_gather | solution.py:55
  71.1 16.6 %all-gather.14.cloned.1.call-done = bf16[1024,1024]{1,0:T(8,128)(2,1)} async-done(((bf16[256,1024]{1,0:T(8,128)(2,1)}), bf16[1024,1024]{1,0:T(8,128)(2,1)}) %all-gather.14.cloned.1.call-update) | async-done | bytes 2097168 | tf_op jit(solution)/shard_map/all_gather | solution.py:132
  92.7 19.8 %all-gather.24.cloned.1.call-done = bf16[1024,1024]{1,0:T(8,128)(2,1)} async-done(((bf16[256,1024]{1,0:T(8,128)(2,1)}), bf16[1024,1024]{1,0:T(8,128)(2,1)}) %all-gather.24.cloned.1.call-update) | async-done | bytes 2097168 | tf_op jit(solution)/shard_map/all_gather | solution.py:132
  168.0 20.9 %all-gather.1 = bf16[8,1,128]{2,1,0:T(2,128)(2,1)S(1)} all-gather(bf16[1,1,128]{2,1,0:T(2,128)(2,1)S(1)} %bitcast.479), channel_id=1, replica_groups=mesh['dp'=8,'mp'=4] {'dp'}, dimensions={0}, use_global_device_ids=true | all-gather | bytes 2304 | tf_op jit(solution)/shard_map/all_gather | solution.py:64
  188.9 43.7 %reduce-scatter.25.cloned.1.call-done = f32[256,1024]{1,0:T(8,128)} async-done(((f32[1024,1024]{1,0:T(8,128)}), f32[256,1024]{1,0:T(8,128)}) %reduce-scatter.25.cloned.1.call-update) | async-done | bytes 1048592 | tf_op jit(solution)/shard_map/reduce_scatter | solution.py:153
  236.9 40.2 %all-gather.22.cloned.1.call-done = bf16[656,1024]{1,0:T(8,128)(2,1)} async-done(((bf16[656,128]{1,0:T(8,128)(2,1)}), bf16[656,1024]{1,0:T(8,128)(2,1)}) %all-gather.22.cloned.1.call-update) | async-done | bytes 1343504 | tf_op jit(solution)/shard_map/all_gather | solution.py:63
  277.1 23.4 %all-gather.32.cloned.1.call-done = bf16[1024,1024]{1,0:T(8,128)(2,1)} async-done(((bf16[256,1024]{1,0:T(8,128)(2,1)}), bf16[1024,1024]{1,0:T(8,128)(2,1)}) %all-gather.32.cloned.1.call-update) | async-done | bytes 2097168 | tf_op jit(solution)/shard_map/all_gather | solution.py:184
  305.7 54.5 %all-gather.20.cloned.1.call-done = bf16[2,1024,656]{1,2,0:T(8,128)(2,1)} async-done(((bf16[2,128,656]{1,2,0:T(8,128)(2,1)}), bf16[2,1024,656]{1,2,0:T(8,128)(2,1)}) %all-gather.20.cloned.1.call-update) | async-done | bytes 2686992 | tf_op jit(solution)/shard_map/all_gather | solution.py:62
  360.2 22.4 %all-gather.26.cloned.1.call-done = bf16[1024,1024]{1,0:T(8,128)(2,1)} async-done(((bf16[256,1024]{1,0:T(8,128)(2,1)}), bf16[1024,1024]{1,0:T(8,128)(2,1)}) %all-gather.26.cloned.1.call-update) | async-done | bytes 2097168 | tf_op jit(solution)/shard_map/all_gather | solution.py:162
  412.3 19.1 %all-gather.18.cloned.1.call-done = bf16[1024,1024]{1,0:T(8,128)(2,1)} async-done(((bf16[256,1024]{1,0:T(8,128)(2,1)}), bf16[1024,1024]{1,0:T(8,128)(2,1)}) %all-gather.18.cloned.1.call-update) | async-done | bytes 2097168 | tf_op jit(solution)/shard_map/all_gather | solution.py:162
  465.2 34.1 %reduce-scatter.29.cloned.1.call-done = bf16[256,1024]{1,0:T(8,128)(2,1)} async-done(((bf16[1024,1024]{1,0:T(8,128)(2,1)}), bf16[256,1024]{1,0:T(8,128)(2,1)}) %reduce-scatter.29.cloned.1.call-update) | async-done | bytes 524304 | tf_op jit(solution)/shard_map/reduce_scatter | solution.py:196
  502.0 31.2 %reduce-scatter.27.cloned.1.call-done = bf16[256,1024]{1,0:T(8,128)(2,1)} async-done(((bf16[1024,1024]{1,0:T(8,128)(2,1)}), bf16[256,1024]{1,0:T(8,128)(2,1)}) %reduce-scatter.27.cloned.1.call-update) | async-done | bytes 524304 | tf_op jit(solution)/shard_map/reduce_scatter | solution.py:168
  533.2 34.0 %reduce-scatter.23.cloned.1.call-done = bf16[256,1024]{1,0:T(8,128)(2,1)} async-done(((bf16[1024,1024]{1,0:T(8,128)(2,1)}), bf16[256,1024]{1,0:T(8,128)(2,1)}) %reduce-scatter.23.cloned.1.call-update) | async-done | bytes 524304 | tf_op jit(solution)/shard_map/reduce_scatter | solution.py:168
  604.5 14.8 %multiply_reduce_fusion.1 = (f32[4,1024]{1,0:T(4,128)S(1)}, f32[4,1024,1024]{1,2,0:T(8,128)}) fusion(f32[4,1024,1024]{1,2,0:T(8,128)} %copy-done.1, f32[4,1024]{1,0:T(4,128)S(1)} %log_add_fusion.1, pred[1024]{0:T(1024)(128)(4,1)S(1)} %iota_compare_fusion.1, bf16[1024,4,64]{0,2,1:T(8,128)(2,1)S(1)} %bitcast.455, bf16[1024,4,64]{0,2,1:T(8,128)(2,1)S(1)} %bitcast.452), kind=kOutput, calls=%fused_computation.3 | convolution fusion | flops 557838336 | bytes 34636800 | tf_op jit(solution)/shard_map/qhd,khd->hqk/dot_general | solution.py:225
  621.1 8.6 multiply_convert_fusion.1
  642.8 15.3 %multiply_reduce_fusion = (f32[4,1024]{1,0:T(4,128)}, f32[4,1024,1024]{1,2,0:T(8,128)}) fusion(f32[4,1024,1024]{1,2,0:T(8,128)} %copy-done, f32[4,1024]{1,0:T(4,128)S(1)} %log_add_fusion, pred[1024]{0:T(1024)(128)(4,1)S(1)} %iota_compare_fusion, bf16[1024,4,64]{0,2,1:T(8,128)(2,1)} %bitcast.457, bf16[1024,4,64]{0,2,1:T(8,128)(2,1)S(1)} %bitcast.454), kind=kOutput, calls=%fused_computation.1 | convolution fusion | flops 557838336 | bytes 34636800 | tf_op jit(solution)/shard_map/qhd,khd->hqk/dot_general | solution.py:225
  659.6 9.1 multiply_convert_fusion
  717.9 44.1 %reduce-scatter.41.cloned.1.call-done = bf16[128,1312]{1,0:T(8,128)(2,1)} async-done(((bf16[1024,1312]{1,0:T(8,128)(2,1)}), bf16[128,1312]{1,0:T(8,128)(2,1)}) %reduce-scatter.41.cloned.1.call-update) | async-done | bytes 335888
  765.0 61.6 %reduce-scatter.39.cloned.1.call-done = bf16[128,256]{1,0:T(8,128)(2,1)} async-done(((bf16[1024,256]{1,0:T(8,128)(2,1)}), bf16[128,256]{1,0:T(8,128)(2,1)}) %reduce-scatter.39.cloned.1.call-update) | async-done | bytes 65552
  828.3 65.6 %reduce-scatter.37.cloned.1.call-done = bf16[128,768]{1,0:T(8,128)(2,1)} async-done(((bf16[1024,768]{1,0:T(8,128)(2,1)}), bf16[128,768]{1,0:T(8,128)(2,1)}) %reduce-scatter.37.cloned.1.call-update) | async-done | bytes 196624
  896.1 30.9 %reduce-scatter.35.cloned.1.call-done = bf16[256,1024]{1,0:T(8,128)(2,1)} async-done(((bf16[1024,1024]{1,0:T(8,128)(2,1)}), bf16[256,1024]{1,0:T(8,128)(2,1)}) %reduce-scatter.35.cloned.1.call-update) | async-done | bytes 524304 | tf_op jit(solution)/shard_map/reduce_scatter | solution.py:250
  927.0 34.0 %reduce-scatter.31.cloned.1.call-done = bf16[256,1024]{1,0:T(8,128)(2,1)} async-done(((bf16[1024,1024]{1,0:T(8,128)(2,1)}), bf16[256,1024]{1,0:T(8,128)(2,1)}) %reduce-scatter.31.cloned.1.call-update) | async-done | bytes 524304 | tf_op jit(solution)/shard_map/reduce_scatter | solution.py:250
  965.2 21.4 %all-reduce.3 = (bf16[1024]{0:T(1024)(128)(2,1)S(1)}, bf16[1024]{0:T(1024)(128)(2,1)S(1)}) all-reduce(bf16[1024]{0:T(1024)(128)(2,1)S(1)} %add_convert_fusion.6, bf16[1024]{0:T(1024)(128)(2,1)S(1)} %add_convert_fusion.5), channel_id=10, replica_groups=mesh['dp'=8,'mp'=4] {'dp'}, use_global_device_ids=true, to_apply=%region_32.33.clone | all-reduce | flops 2048 | bytes 8192
  (389 shorter events, 268.8 us)
Async XLA Ops:
  7.2 64.0 %all-gather.16.cloned.1.call-start = ((), (), s32[]{:S(2)}) async-start(), calls=%async_computation.13 | async-start | bytes 1769472 | tf_op jit(solution)/shard_map/all_gather | solution.py:54
  9.1 78.7 %all-gather.14.cloned.1.call-start = ((), (), s32[]{:S(2)}) async-start(), calls=%async_computation.12 | async-start | bytes 2621440 | tf_op jit(solution)/shard_map/all_gather | solution.py:132
  36.5 76.1 %all-gather.24.cloned.1.call-start = ((), (), s32[]{:S(2)}) async-start(), calls=%async_computation.19 | async-start | bytes 2621440 | tf_op jit(solution)/shard_map/all_gather | solution.py:132
  37.2 151.7 %reduce-scatter.21.cloned.1.call-start = ((), (), s32[]{:S(2)}) async-start(), calls=%async_computation.14 | async-start | bytes 5242880 | tf_op jit(solution)/shard_map/reduce_scatter | solution.py:153
  140.8 91.7 %reduce-scatter.25.cloned.1.call-start = ((), (), s32[]{:S(2)}) async-start(), calls=%async_computation.20 | async-start | bytes 5242880 | tf_op jit(solution)/shard_map/reduce_scatter | solution.py:153
  164.0 113.1 %all-gather.22.cloned.1.call-start = ((), (), s32[]{:S(2)}) async-start(), calls=%async_computation.17 | async-start | bytes 1511424 | tf_op jit(solution)/shard_map/all_gather | solution.py:63
  164.6 135.9 %all-gather.32.cloned.1.call-start = ((), (), s32[]{:S(2)}) async-start(), calls=%async_computation.27 | async-start | bytes 2621440 | tf_op jit(solution)/shard_map/all_gather | solution.py:184
  165.9 404.6 %copy-start.65 = (f32[256]{0:T(256)}, f32[256]{0:T(256)S(1)}, u32[]{:S(2)}) copy-start(f32[256]{0:T(256)S(1)} %get-tuple-element.125) | copy-start | bytes 3076
  167.2 193.0 %all-gather.20.cloned.1.call-start = ((), (), s32[]{:S(2)}) async-start(), calls=%async_computation.16 | async-start | bytes 3022848 | tf_op jit(solution)/shard_map/all_gather | solution.py:62
  167.9 214.7 %all-gather.26.cloned.1.call-start = ((), (), s32[]{:S(2)}) async-start(), calls=%async_computation.21 | async-start | bytes 2621440 | tf_op jit(solution)/shard_map/all_gather | solution.py:162
  236.3 170.9 %all-gather.28.cloned.1.call-start = ((), (), s32[]{:S(2)}) async-start(), calls=%async_computation.23 | async-start | bytes 2621440 | tf_op jit(solution)/shard_map/all_gather | solution.py:184
  236.9 194.5 %all-gather.18.cloned.1.call-start = ((), (), s32[]{:S(2)}) async-start(), calls=%async_computation.15 | async-start | bytes 2621440 | tf_op jit(solution)/shard_map/all_gather | solution.py:162
  305.6 159.6 %reduce-scatter.33.cloned.1.call-start = ((), (), s32[]{:S(2)}) async-start(), calls=%async_computation.28 | async-start | bytes 2621440 | tf_op jit(solution)/shard_map/reduce_scatter | solution.py:196
  403.0 96.4 %reduce-scatter.29.cloned.1.call-start = ((), (), s32[]{:S(2)}) async-start(), calls=%async_computation.24 | async-start | bytes 2621440 | tf_op jit(solution)/shard_map/reduce_scatter | solution.py:196
  451.7 81.5 %reduce-scatter.27.cloned.1.call-start = ((), (), s32[]{:S(2)}) async-start(), calls=%async_computation.22 | async-start | bytes 2621440 | tf_op jit(solution)/shard_map/reduce_scatter | solution.py:168
  456.7 110.5 %reduce-scatter.23.cloned.1.call-start = ((), (), s32[]{:S(2)}) async-start(), calls=%async_computation.18 | async-start | bytes 2621440 | tf_op jit(solution)/shard_map/reduce_scatter | solution.py:168
  461.7 139.3 %all-gather.30.cloned.1.call-start = ((), (), s32[]{:S(2)}) async-start(), calls=%async_computation.25 | async-start | bytes 2621440 | tf_op jit(solution)/shard_map/all_gather | solution.py:207
  572.2 63.7 %all-gather.34.cloned.1.call-start = ((), (), s32[]{:S(2)}) async-start(), calls=%async_computation.29 | async-start | bytes 2621440 | tf_op jit(solution)/shard_map/all_gather | solution.py:207
  572.8 142.1 %reduce-scatter.43.cloned.1.call-start = ((), (), s32[]{:S(2)}) async-start(), calls=%async_computation.34 | async-start | bytes 1769472
  579.4 182.6 %reduce-scatter.41.cloned.1.call-start = ((), (), s32[]{:S(2)}) async-start(), calls=%async_computation.33 | async-start | bytes 3244032
  601.0 225.7 %reduce-scatter.39.cloned.1.call-start = ((), (), s32[]{:S(2)}) async-start(), calls=%async_computation.32 | async-start | bytes 589824
  684.1 209.8 %reduce-scatter.37.cloned.1.call-start = ((), (), s32[]{:S(2)}) async-start(), calls=%async_computation.31 | async-start | bytes 1769472
  705.0 222.0 %reduce-scatter.35.cloned.1.call-start = ((), (), s32[]{:S(2)}) async-start(), calls=%async_computation.30 | async-start | bytes 2621440 | tf_op jit(solution)/shard_map/reduce_scatter | solution.py:250
  710.2 250.7 %reduce-scatter.31.cloned.1.call-start = ((), (), s32[]{:S(2)}) async-start(), calls=%async_computation.26 | async-start | bytes 2621440 | tf_op jit(solution)/shard_map/reduce_scatter | solution.py:250
  (101 other events, 2683.0 us)
Sparse Core Ops, SparseCore 0:
  10.6 51.3 all-gather.15
  64.2 23.5 all-gather.13
  89.9 22.5 all-gather.23
  141.0 44.5 reduce-scatter.20
  188.1 44.4 reduce-scatter.24
  234.5 42.5 all-gather.21
  279.3 21.2 all-gather.31
  302.5 57.6 all-gather.19
  361.8 20.7 all-gather.25
  384.6 22.5 all-gather.27
  408.8 22.5 all-gather.17
  433.8 31.4 reduce-scatter.32
  467.9 31.3 reduce-scatter.28
  501.7 31.4 reduce-scatter.26
  535.7 31.3 reduce-scatter.22
  572.3 22.6 all-gather.29
  596.4 22.5 all-gather.33
  622.3 64.7 reduce-scatter.42
  691.1 70.9 reduce-scatter.40
  765.6 61.0 reduce-scatter.38
  830.1 63.7 reduce-scatter.36
  896.6 30.3 reduce-scatter.34
  929.5 31.3 reduce-scatter.30
where the time goes:
time: 1010 us; the launch traced here: 1000 us
  waiting for transfers between devices  586 us (58%)
  matrix products  149 us (15%)
  blocking collectives  102 us (10%)
  other arithmetic  96 us (10%)
  local copies, waits for them, and re-layouts  53.1 us (5%)
  between operations  16.4 us (2%)
    unnamed x27, waiting for transfers between devices  175 us
    reduce_scatter x2, waiting for transfers between devices, per_device(): lax.psum_scatter(jnp.dot(mixed_rows, ffn_out_full, preferred_element_type...  65.2 us
    reduce_scatter x2, waiting for transfers between devices, per_device(): lax.psum_scatter(jnp.einsum('cle,cde->ld', projected_back, qkv_full, pref...  64.9 us
    all_gather x1, waiting for transfers between devices, fetch_feedforward(): lax.all_gather(ffn_in_weight, 'dp', axis=1, tiled=True)  54.5 us
    unnamed x219, local copies, waits for them, and re-layouts  46.2 us
    reduce_scatter x2, waiting for transfers between devices, per_device(): lax.psum_scatter(jnp.dot(context, attn_out_full, preferred_element_type=j...  43.7 us
    all_gather x2, waiting for transfers between devices, per_device(): full_two = lax.all_gather(normed_two, 'mp', axis=0, tiled=True)  41.5 us
    all_gather x1, waiting for transfers between devices, fetch_feedforward(): lax.all_gather(ffn_out_weight, 'dp', axis=1, tiled=True)  40.2 us
  transfers between devices with their start and end apart: 23, of which 18 were waited for; matrix products, arithmetic and copies ran while one was open for 24% of the time, Pallas kernels for 0%

commit v1 on v0

--- a/solution.py
+++ b/solution.py
@@ -6,6 +6,18 @@
 HD = 64
 norm_eps = 1e-05
 rope_base = 160000.0
+
+
+def gather_by_bits(x, axis, dim):
+    ways, here = (lax.axis_size(axis), lax.axis_index(axis))
+    grown, reach = (x, 1)
+    while reach < ways:
+        theirs = lax.ppermute(grown, axis, [(d, d ^ reach) for d in range(ways)])
+        mine_first = jnp.concatenate([grown, theirs], axis=dim)
+        theirs_first = jnp.concatenate([theirs, grown], axis=dim)
+        grown = jnp.where(here & reach == 0, mine_first, theirs_first)
+        reach = 2 * reach
+    return grown
 
 
 def layer_norm(values, norm_gain):
@@ -59,7 +71,7 @@
 
 def fetch_feedforward(ffn_in_weight, ffn_out_weight, ffn_norm):
     return (
-        lax.all_gather(ffn_in_weight, "dp", axis=1, tiled=True),
+        gather_by_bits(ffn_in_weight, "dp", 1),
         lax.all_gather(ffn_out_weight, "dp", axis=1, tiled=True),
         lax.all_gather(ffn_norm, "dp", axis=0, tiled=True),
     )

time: 1010 us -> 1050 us (1.040)
  waiting for transfers between devices: 586 us -> 598 us
    ppermute x0 -> x3, waiting for transfers between devices: none -> 31 us  [gather_by_bits(): theirs = lax.ppermute(grown, axis, [(d, d ^ reach) for d in range(ways)])]
    unnamed x27, waiting for transfers between devices: 175 us -> 162 us
    all_gather x2, waiting for transfers between devices: 27.2 us -> 38.7 us  [per_device(): lax.all_gather(out_back.astype(jnp.bfloat16), 'mp', axis=0, tiled=True)]
    all_gather x1, waiting for transfers between devices: 54.5 us -> 43.7 us  [fetch_feedforward_again(): lax.all_gather(ffn_in_weight, 'dp', axis=1, tiled=True)]
    unnamed x219 -> x225, local copies, waits for them, and re-layouts: 46.2 us -> 46.4 us
  transfers between devices with their start and end apart: 23 -> 26, of which waited for: 18 -> 20; matrix products, arithmetic and copies ran while one was open for 24% -> 25% of each run, Pallas kernels for 0% -> 0%
where the time goes in v1:
time: 1050 us; the launch traced here: 1040 us
  waiting for transfers between devices  598 us (57%)
  matrix products  159 us (15%)
  other arithmetic  103 us (10%)
  blocking collectives  102 us (10%)
  local copies, waits for them, and re-layouts  54.7 us (5%)
  between operations  16.5 us (2%)
    unnamed x27, waiting for transfers between devices  162 us
    reduce_scatter x2, waiting for transfers between devices, per_device(): lax.psum_scatter(jnp.dot(mixed_rows, ffn_out_full, preferred_element_type...  65.2 us
    reduce_scatter x2, waiting for transfers between devices, per_device(): lax.psum_scatter(jnp.einsum('cle,cde->ld', projected_back, qkv_full, pref...  64.9 us
    unnamed x225, local copies, waits for them, and re-layouts  46.4 us
    reduce_scatter x2, waiting for transfers between devices, per_device(): lax.psum_scatter(jnp.dot(context, attn_out_full, preferred_element_type=j...  44.4 us
    all_gather x1, waiting for transfers between devices, fetch_feedforward_again(): lax.all_gather(ffn_in_weight, 'dp', axis=1, tiled=True)  43.7 us
    all_gather x2, waiting for transfers between devices, per_device(): lax.all_gather(out_back.astype(jnp.bfloat16), 'mp', axis=0, tiled=True)  38.7 us
    all_gather x2, waiting for transfers between devices, per_device(): full_two = lax.all_gather(normed_two, 'mp', axis=0, tiled=True)  38.2 us
  transfers between devices with their start and end apart: 26, of which 20 were waited for; matrix products, arithmetic and copies ran while one was open for 25% of the time, Pallas kernels for 0%

profile of v1, /device:TPU:0, one launch (start us, length us, event | category | flops | bytes accessed | tf_op | source)
XLA Modules:
  0.0 1041.1 jit_solution(6290410844251133537)
XLA Ops:
  9.1 22.3 %all-gather = bf16[8,1,128]{2,1,0:T(2,128)(2,1)S(1)} all-gather(bf16[1,1,128]{2,1,0:T(2,128)(2,1)} %bitcast.476), channel_id=1, replica_groups=mesh['dp'=8,'mp'=4] {'dp'}, dimensions={0}, use_global_device_ids=true | all-gather | bytes 2304 | tf_op jit(solution)/shard_map/all_gather | solution.py:68
  40.4 30.7 %all_gather.57 = bf16[256,1024]{1,0:T(8,128)(2,1)} all-gather(bf16[256,128]{1,0:T(8,128)(2,1)S(1)} %copy-done.62), channel_id=1, replica_groups=mesh['dp'=8,'mp'=4] {'dp'}, dimensions={1}, use_global_device_ids=true | all-gather | bytes 589824 | tf_op jit(solution)/shard_map/all_gather | solution.py:67
  71.2 16.4 %all-gather.22.cloned.1.call-done = bf16[1024,1024]{1,0:T(8,128)(2,1)} async-done(((bf16[256,1024]{1,0:T(8,128)(2,1)}), bf16[1024,1024]{1,0:T(8,128)(2,1)}) %all-gather.22.cloned.1.call-update) | async-done | bytes 2097168 | tf_op jit(solution)/shard_map/all_gather | solution.py:144
  92.6 19.8 %all-gather.14.cloned.1.call-done = bf16[1024,1024]{1,0:T(8,128)(2,1)} async-done(((bf16[256,1024]{1,0:T(8,128)(2,1)}), bf16[1024,1024]{1,0:T(8,128)(2,1)}) %all-gather.14.cloned.1.call-update) | async-done | bytes 2097168 | tf_op jit(solution)/shard_map/all_gather | solution.py:144
  167.2 20.9 %all-gather.1 = bf16[8,1,128]{2,1,0:T(2,128)(2,1)S(1)} all-gather(bf16[1,1,128]{2,1,0:T(2,128)(2,1)S(1)} %bitcast.477), channel_id=1, replica_groups=mesh['dp'=8,'mp'=4] {'dp'}, dimensions={0}, use_global_device_ids=true | all-gather | bytes 2304 | tf_op jit(solution)/shard_map/all_gather | solution.py:76
  188.1 44.4 %reduce-scatter.21.cloned.1.call-done = f32[256,1024]{1,0:T(8,128)} async-done(((f32[1024,1024]{1,0:T(8,128)}), f32[256,1024]{1,0:T(8,128)}) %reduce-scatter.21.cloned.1.call-update) | async-done | bytes 1048592 | tf_op jit(solution)/shard_map/reduce_scatter | solution.py:165
  250.8 21.1 %collective-permute-done.1 = bf16[2,256,656]{1,2,0:T(8,128)(2,1)} collective-permute-done((bf16[2,256,656]{1,2,0:T(8,128)(2,1)S(1)}, bf16[2,256,656]{1,2,0:T(8,128)(2,1)}, u32[]{:S(2)}, u32[]{:S(2)}) %collective-permute-start.1) | collective-permute-done | bytes 671776 | tf_op jit(solution)/shard_map/ppermute | solution.py:15
  277.7 36.4 %all-gather.20.cloned.1.call-done = bf16[656,1024]{1,0:T(8,128)(2,1)} async-done(((bf16[656,128]{1,0:T(8,128)(2,1)}), bf16[656,1024]{1,0:T(8,128)(2,1)}) %all-gather.20.cloned.1.call-update) | async-done | bytes 1343504 | tf_op jit(solution)/shard_map/all_gather | solution.py:75
  314.1 23.7 %all-gather.26.cloned.1.call-done = bf16[1024,1024]{1,0:T(8,128)(2,1)} async-done(((bf16[256,1024]{1,0:T(8,128)(2,1)}), bf16[1024,1024]{1,0:T(8,128)(2,1)}) %all-gather.26.cloned.1.call-update) | async-done | bytes 2097168 | tf_op jit(solution)/shard_map/all_gather | solution.py:196
  343.0 19.0 %all-gather.18.cloned.1.call-done = bf16[1024,1024]{1,0:T(8,128)(2,1)} async-done(((bf16[256,1024]{1,0:T(8,128)(2,1)}), bf16[1024,1024]{1,0:T(8,128)(2,1)}) %all-gather.18.cloned.1.call-update) | async-done | bytes 2097168 | tf_op jit(solution)/shard_map/all_gather | solution.py:174
  378.0 43.7 %all-gather.28.cloned.1.call-done = bf16[2,1024,656]{1,2,0:T(8,128)(2,1)} async-done(((bf16[2,128,656]{1,2,0:T(8,128)(2,1)}), bf16[2,1024,656]{1,2,0:T(8,128)(2,1)}) %all-gather.28.cloned.1.call-update) | async-done | bytes 2686992 | tf_op jit(solution)/shard_map/all_gather | solution.py:90
  429.6 15.0 %all-gather.32.cloned.1.call-done = bf16[1024,1024]{1,0:T(8,128)(2,1)} async-done(((bf16[256,1024]{1,0:T(8,128)(2,1)}), bf16[1024,1024]{1,0:T(8,128)(2,1)}) %all-gather.32.cloned.1.call-update) | async-done | bytes 2097168 | tf_op jit(solution)/shard_map/all_gather | solution.py:196
  449.6 19.1 %all-gather.24.cloned.1.call-done = bf16[1024,1024]{1,0:T(8,128)(2,1)} async-done(((bf16[256,1024]{1,0:T(8,128)(2,1)}), bf16[1024,1024]{1,0:T(8,128)(2,1)}) %all-gather.24.cloned.1.call-update) | async-done | bytes 2097168 | tf_op jit(solution)/shard_map/all_gather | solution.py:174
  502.6 34.1 %reduce-scatter.33.cloned.1.call-done = bf16[256,1024]{1,0:T(8,128)(2,1)} async-done(((bf16[1024,1024]{1,0:T(8,128)(2,1)}), bf16[256,1024]{1,0:T(8,128)(2,1)}) %reduce-scatter.33.cloned.1.call-update) | async-done | bytes 524304 | tf_op jit(solution)/shard_map/reduce_scatter | solution.py:208
  539.3 31.2 %reduce-scatter.23.cloned.1.call-done = bf16[256,1024]{1,0:T(8,128)(2,1)} async-done(((bf16[1024,1024]{1,0:T(8,128)(2,1)}), bf16[256,1024]{1,0:T(8,128)(2,1)}) %reduce-scatter.23.cloned.1.call-update) | async-done | bytes 524304 | tf_op jit(solution)/shard_map/reduce_scatter | solution.py:180
  570.5 34.0 %reduce-scatter.27.cloned.1.call-done = bf16[256,1024]{1,0:T(8,128)(2,1)} async-done(((bf16[1024,1024]{1,0:T(8,128)(2,1)}), bf16[256,1024]{1,0:T(8,128)(2,1)}) %reduce-scatter.27.cloned.1.call-update) | async-done | bytes 524304 | tf_op jit(solution)/shard_map/reduce_scatter | solution.py:180
  643.1 14.9 %multiply_reduce_fusion.1 = (f32[4,1024]{1,0:T(4,128)S(1)}, f32[4,1024,1024]{1,2,0:T(8,128)}) fusion(f32[4,1024,1024]{1,2,0:T(8,128)} %copy-done.1, f32[4,1024]{1,0:T(4,128)S(1)} %log_add_fusion.1, pred[1024]{0:T(1024)(128)(4,1)S(1)} %iota_compare_fusion.1, bf16[1024,4,64]{0,2,1:T(8,128)(2,1)S(1)} %bitcast.453, bf16[1024,4,64]{0,2,1:T(8,128)(2,1)S(1)} %bitcast.452), kind=kOutput, calls=%fused_computation.3 | convolution fusion | flops 557838336 | bytes 34636800 | tf_op jit(solution)/shard_map/qhd,khd->hqk/dot_general | solution.py:237
  681.3 15.3 %multiply_reduce_fusion = (f32[4,1024]{1,0:T(4,128)}, f32[4,1024,1024]{1,2,0:T(8,128)}) fusion(f32[4,1024,1024]{1,2,0:T(8,128)} %copy-done, f32[4,1024]{1,0:T(4,128)S(1)} %copy-done.59, pred[1024]{0:T(1024)(128)(4,1)S(1)} %copy-done.64, bf16[1024,4,64]{0,2,1:T(8,128)(2,1)} %bitcast.455, bf16[1024,4,64]{0,2,1:T(8,128)(2,1)S(1)} %bitcast.450), kind=kOutput, calls=%fused_computation.1 | convolution fusion | flops 557838336 | bytes 34636800 | tf_op jit(solution)/shard_map/qhd,khd->hqk/dot_general | solution.py:237
  768.1 31.3 %reduce-scatter.41.cloned.1.call-done = bf16[128,1312]{1,0:T(8,128)(2,1)} async-done(((bf16[1024,1312]{1,0:T(8,128)(2,1)}), bf16[128,1312]{1,0:T(8,128)(2,1)}) %reduce-scatter.41.cloned.1.call-update) | async-done | bytes 335888
  802.4 61.7 %reduce-scatter.39.cloned.1.call-done = bf16[128,256]{1,0:T(8,128)(2,1)} async-done(((bf16[1024,256]{1,0:T(8,128)(2,1)}), bf16[128,256]{1,0:T(8,128)(2,1)}) %reduce-scatter.39.cloned.1.call-update) | async-done | bytes 65552
  865.7 65.6 %reduce-scatter.37.cloned.1.call-done = bf16[128,768]{1,0:T(8,128)(2,1)} async-done(((bf16[1024,768]{1,0:T(8,128)(2,1)}), bf16[128,768]{1,0:T(8,128)(2,1)}) %reduce-scatter.37.cloned.1.call-update) | async-done | bytes 196624
  933.5 30.9 %reduce-scatter.35.cloned.1.call-done = bf16[256,1024]{1,0:T(8,128)(2,1)} async-done(((bf16[1024,1024]{1,0:T(8,128)(2,1)}), bf16[256,1024]{1,0:T(8,128)(2,1)}) %reduce-scatter.35.cloned.1.call-update) | async-done | bytes 524304 | tf_op jit(solution)/shard_map/reduce_scatter | solution.py:262
  964.4 34.0 %reduce-scatter.31.cloned.1.call-done = bf16[256,1024]{1,0:T(8,128)(2,1)} async-done(((bf16[1024,1024]{1,0:T(8,128)(2,1)}), bf16[256,1024]{1,0:T(8,128)(2,1)}) %reduce-scatter.31.cloned.1.call-update) | async-done | bytes 524304 | tf_op jit(solution)/shard_map/reduce_scatter | solution.py:262
  1002.7 21.4 %all-reduce.3 = (bf16[1024]{0:T(1024)(128)(2,1)S(1)}, bf16[1024]{0:T(1024)(128)(2,1)S(1)}) all-reduce(bf16[1024]{0:T(1024)(128)(2,1)S(1)} %add_convert_fusion.6, bf16[1024]{0:T(1024)(128)(2,1)S(1)} %add_convert_fusion.5), channel_id=10, replica_groups=mesh['dp'=8,'mp'=4] {'dp'}, use_global_device_ids=true, to_apply=%region_32.33.clone | all-reduce | flops 2048 | bytes 8192
  (403 shorter events, 317.8 us)
Async XLA Ops:
  7.2 64.0 %all-gather.16.cloned.1.call-start = ((), (), s32[]{:S(2)}) async-start(), calls=%async_computation.13 | async-start | bytes 1769472 | tf_op jit(solution)/shard_map/all_gather | solution.py:66
  9.1 78.5 %all-gather.22.cloned.1.call-start = ((), (), s32[]{:S(2)}) async-start(), calls=%async_computation.18 | async-start | bytes 2621440 | tf_op jit(solution)/shard_map/all_gather | solution.py:144
  36.6 75.8 %all-gather.14.cloned.1.call-start = ((), (), s32[]{:S(2)}) async-start(), calls=%async_computation.12 | async-start | bytes 2621440 | tf_op jit(solution)/shard_map/all_gather | solution.py:144
  37.3 150.8 %reduce-scatter.25.cloned.1.call-start = ((), (), s32[]{:S(2)}) async-start(), calls=%async_computation.19 | async-start | bytes 5242880 | tf_op jit(solution)/shard_map/reduce_scatter | solution.py:165
  140.7 91.7 %reduce-scatter.21.cloned.1.call-start = ((), (), s32[]{:S(2)}) async-start(), calls=%async_computation.14 | async-start | bytes 5242880 | tf_op jit(solution)/shard_map/reduce_scatter | solution.py:165
  163.9 150.2 %all-gather.20.cloned.1.call-start = ((), (), s32[]{:S(2)}) async-start(), calls=%async_computation.16 | async-start | bytes 1511424 | tf_op jit(solution)/shard_map/all_gather | solution.py:75
  164.5 173.4 %all-gather.26.cloned.1.call-start = ((), (), s32[]{:S(2)}) async-start(), calls=%async_computation.22 | async-start | bytes 2621440 | tf_op jit(solution)/shard_map/all_gather | solution.py:196
  167.1 194.9 %all-gather.18.cloned.1.call-start = ((), (), s32[]{:S(2)}) async-start(), calls=%async_computation.15 | async-start | bytes 2621440 | tf_op jit(solution)/shard_map/all_gather | solution.py:174
  236.1 185.6 %all-gather.28.cloned.1.call-start = ((), (), s32[]{:S(2)}) async-start(), calls=%async_computation.23 | async-start | bytes 3022848 | tf_op jit(solution)/shard_map/all_gather | solution.py:90
  236.9 207.7 %all-gather.32.cloned.1.call-start = ((), (), s32[]{:S(2)}) async-start(), calls=%async_computation.27 | async-start | bytes 2621440 | tf_op jit(solution)/shard_map/all_gather | solution.py:196
  237.5 231.3 %all-gather.24.cloned.1.call-start = ((), (), s32[]{:S(2)}) async-start(), calls=%async_computation.20 | async-start | bytes 2621440 | tf_op jit(solution)/shard_map/all_gather | solution.py:174
  274.6 68.4 %collective-permute-start.2 = (bf16[2,512,656]{1,2,0:T(8,128)(2,1)}, bf16[2,512,656]{1,2,0:T(8,128)(2,1)}, u32[]{:S(2)}, u32[]{:S(2)}) collective-permute-start(bf16[2,512,656]{1,2,0:T(8,128)(2,1)} %maximum_select_fusion.1), channel_id=1, source_target_pairs={{0,16},{4,20},{8,24},{12,28},{16,0},{20,4},{24,8},{28,12},{1,17},{... | collective-permute-start | bytes 4030472 | tf_op jit(solution)/shard_map/ppermute | solution.py:15
  342.9 159.7 %reduce-scatter.29.cloned.1.call-start = ((), (), s32[]{:S(2)}) async-start(), calls=%async_computation.24 | async-start | bytes 2621440 | tf_op jit(solution)/shard_map/reduce_scatter | solution.py:208
  429.1 107.6 %reduce-scatter.33.cloned.1.call-start = ((), (), s32[]{:S(2)}) async-start(), calls=%async_computation.28 | async-start | bytes 2621440 | tf_op jit(solution)/shard_map/reduce_scatter | solution.py:208
  489.4 81.1 %reduce-scatter.23.cloned.1.call-start = ((), (), s32[]{:S(2)}) async-start(), calls=%async_computation.17 | async-start | bytes 2621440 | tf_op jit(solution)/shard_map/reduce_scatter | solution.py:180
  494.4 110.1 %reduce-scatter.27.cloned.1.call-start = ((), (), s32[]{:S(2)}) async-start(), calls=%async_computation.21 | async-start | bytes 2621440 | tf_op jit(solution)/shard_map/reduce_scatter | solution.py:180
  499.3 140.2 %all-gather.30.cloned.1.call-start = ((), (), s32[]{:S(2)}) async-start(), calls=%async_computation.25 | async-start | bytes 2621440 | tf_op jit(solution)/shard_map/all_gather | solution.py:219
  609.6 64.7 %all-gather.34.cloned.1.call-start = ((), (), s32[]{:S(2)}) async-start(), calls=%async_computation.29 | async-start | bytes 2621440 | tf_op jit(solution)/shard_map/all_gather | solution.py:219
  610.2 154.9 %reduce-scatter.43.cloned.1.call-start = ((), (), s32[]{:S(2)}) async-start(), calls=%async_computation.34 | async-start | bytes 1769472
  619.0 180.4 %reduce-scatter.41.cloned.1.call-start = ((), (), s32[]{:S(2)}) async-start(), calls=%async_computation.33 | async-start | bytes 3244032
  639.5 224.6 %reduce-scatter.39.cloned.1.call-start = ((), (), s32[]{:S(2)}) async-start(), calls=%async_computation.32 | async-start | bytes 589824
  732.6 198.7 %reduce-scatter.37.cloned.1.call-start = ((), (), s32[]{:S(2)}) async-start(), calls=%async_computation.31 | async-start | bytes 1769472
  755.2 209.2 %reduce-scatter.35.cloned.1.call-start = ((), (), s32[]{:S(2)}) async-start(), calls=%async_computation.30 | async-start | bytes 2621440 | tf_op jit(solution)/shard_map/reduce_scatter | solution.py:262
  760.5 237.9 %reduce-scatter.31.cloned.1.call-start = ((), (), s32[]{:S(2)}) async-start(), calls=%async_computation.26 | async-start | bytes 2621440 | tf_op jit(solution)/shard_map/reduce_scatter | solution.py:262
  (107 other events, 3237.7 us)
Sparse Core Ops, SparseCore 0:
  10.1 50.8 all-gather.15
  63.1 24.4 all-gather.21
  89.7 22.5 all-gather.13
  140.8 44.5 reduce-scatter.24
  187.9 44.4 reduce-scatter.20
  234.3 79.7 all-gather.19
  316.2 21.5 all-gather.25
  339.4 22.5 all-gather.17
  364.1 57.6 all-gather.27
  423.7 20.7 all-gather.31
  446.1 22.5 all-gather.23
  471.1 31.4 reduce-scatter.28
  505.3 31.3 reduce-scatter.32
  539.1 31.4 reduce-scatter.22
  573.1 31.3 reduce-scatter.26
  609.8 22.6 all-gather.29
  633.8 22.5 all-gather.33
  659.7 64.7 reduce-scatter.42
  728.5 70.9 reduce-scatter.40
  803.0 61.0 reduce-scatter.38
  867.5 63.7 reduce-scatter.36
  934.0 30.3 reduce-scatter.34
  966.9 31.4 reduce-scatter.30
